TPU v7x, 32 devices: a whole 2x2x4 slice. The times are simulated.
32 devices in a mesh: layer: 2 (over y), row: 4 (over z), col: 4 (over x, core).
Axes of the slice: x: 2, y: 2, z: 4, core: 2. Of those that a mesh axis runs over, the one named last changes fastest.
Arguments:
- right_side: float32 [16, 4, 64, 128], P(None, 'row', 'layer'), may hold values from -6 to 6
- below: float32 [2, 16, 4, 64, 128], P('layer', None, 'row'), may hold values from -4 to 4
- diag_inverse: float32 [4, 4, 4, 4, 4, 128, 128], P(None, None, 'row', None, 'col'), as said below
- factor_blocks: float32 [4, 4, 4, 128, 128], P('row', 'col'), may hold values from -0.125 to 0.125
- block_row: int32 [4, 4, 4], P('row', 'col'), may hold values from 16 to 63, as said below
- block_col: int32 [4, 4, 4], P('row', 'col'), may hold values from 0 to 47, as said below
Outputs:
- solution: float32 [16, 4, 64, 128], P(None, 'row', 'layer')
Inputs may be any that keep to these rules, and one draw needn't show every extreme that they name: block_row[r, c, n] % 4 == r. block_col[r, c, n] % 4 == c, and block_col[r, c, n] // 16 < block_row[r, c, n] // 16. `diag_inverse`: blocks with k < m are zero and blocks with k == m are lower triangular; the diagonal entries of the diagonal blocks lie in 0.5 to 1.5; the other entries below the diagonal are of mean zero with a spread of about 0.5 / sqrt(128) inside the diagonal blocks and 0.5 / sqrt(2048) in the blocks with k > m, not bounded.
All inputs are finite; a program needn't handle non-finite values.
Results may differ from a plain program's by a relative error of at most 0.0001.
Values sent between devices are 32-bit elements; how exact they have to be, the bound alone decides.
A program may use at most 64 MiB of HBM per device.

v0:
```python
import jax
import jax.numpy as jnp
from jax import lax
from jax.sharding import PartitionSpec as P

BLK = 128
NB = 16
STEPS = 4


def body(right_side, below, diag_inverse, factor_blocks, block_row, block_col):
    rows_count = lax.axis_size("row")
    cols_count = lax.axis_size("col")
    col_self = lax.axis_index("col")
    own_rhs = right_side[:, 0]
    local_rows = own_rhs.shape[0]
    rhs_width = own_rhs.shape[1]
    each_supernode_list = NB // rows_count
    col_width = NB // cols_count
    listed = factor_blocks[0, 0]
    row_index = block_row[0, 0]
    col_index = block_col[0, 0]
    row_onehot = (row_index[:, None] // rows_count == jnp.arange(local_rows)[None, :]).astype(
        jnp.float32
    )
    inverted_diagonal = diag_inverse[:, :, 0, :, 0]
    merged = own_rhs - lax.psum_scatter(below[0, :, 0], "layer", scatter_dimension=1, tiled=True)
    accumulated = jnp.zeros_like(own_rhs)
    solved_pieces = []
    for current_supernode in range(STEPS):
        first_row = current_supernode * each_supernode_list
        last_row = first_row + each_supernode_list
        merged_part = merged[first_row:last_row]
        offset = col_index - current_supernode * NB
        active = ((offset >= 0) & (offset < NB)).astype(jnp.float32)
        summed = lax.psum(accumulated[first_row:last_row], "col")
        target_rows = merged_part - summed
        relayed = lax.all_gather(target_rows[:, None], "row", axis=1, tiled=True).reshape(
            NB, rhs_width, BLK
        )
        local_target_rows = lax.dynamic_index_in_dim(
            relayed.reshape(col_width, cols_count, rhs_width, BLK), col_self, 1, keepdims=False
        )
        partial_solved = jnp.einsum(
            "exnc,xvc->evn",
            inverted_diagonal[current_supernode],
            local_target_rows,
            precision=lax.Precision.HIGHEST,
        )
        solved_own = lax.psum(partial_solved, "col")
        if current_supernode + 1 < STEPS:
            solved_all = lax.all_gather(solved_own[:, None], "row", axis=1, tiled=True).reshape(
                NB, rhs_width, BLK
            )
            chosen = jnp.take(solved_all, jnp.clip(offset, 0, NB - 1), axis=0)
        solved_pieces.append(solved_own)
        if current_supernode + 1 < STEPS:
            products = jnp.einsum("nrb,nab->nra", chosen, listed, precision=lax.Precision.HIGHEST)
            accumulated = accumulated + jnp.einsum(
                "nq,nra->qra",
                row_onehot * active[:, None],
                products,
                precision=lax.Precision.HIGHEST,
            )
    solution = jnp.concatenate(solved_pieces, axis=0)
    return solution[:, None]


def solution(mesh):
    return jax.shard_map(
        body,
        mesh=mesh,
        in_specs=(
            P(None, "row", "layer", None),
            P("layer", None, "row", None, None),
            P(None, None, "row", None, "col", None, None),
            P("row", "col", None, None, None),
            P("row", "col", None),
            P("row", "col", None),
        ),
        out_specs=P(None, "row", "layer", None),
        check_vma=False,
    )
```

profile of v0, /device:TPU:0, one launch (start us, length us, event | category | flops | bytes accessed | tf_op | source)
XLA Modules:
  0.0 379.0 jit_solution(7818879516390627955)
XLA Ops:
  6.5 2.2 copy.56
  10.8 16.2 %reduce-scatter.2.cloned.1.call-done = f32[16,32,128]{2,0,1:T(8,128)} async-done(((f32[16,64,128]{2,0,1:T(8,128)}), f32[16,32,128]{2,0,1:T(8,128)}) %reduce-scatter.2.cloned.1.call-update) | async-done | bytes 262160 | tf_op jit(solution)/shard_map/reduce_scatter | solution.py:27
  27.0 1.2 bitcast_subtract_fusion
  28.2 13.9 %all-gather = f32[4,128,128]{2,0,1:T(4,128)S(1)} all-gather(f32[4,32,128]{2,0,1:T(4,128)S(1)} %slice.55), channel_id=2, replica_groups=mesh['layer'=2,'row'=4,'col'=4] {'row'}, dimensions={1}, use_global_device_ids=true | all-gather | bytes 327680 | tf_op jit(solution)/shard_map/all_gather | solution.py:38
  42.1 2.9 convolution_bitcast_fusion.3
  45.1 32.2 %all-reduce.8.cloned.1.call-done = f32[4,32,128]{2,1,0:T(8,128)} async-done(((f32[4,32,128]{2,1,0:T(8,128)}), f32[4,32,128]{2,1,0:T(8,128)}) %all-reduce.8.cloned.1.call-update) | async-done | bytes 65552 | tf_op jit(solution)/shard_map/psum | solution.py:50
  77.3 14.1 %all-gather.1 = f32[4,128,128]{2,1,0:T(8,128)S(1)} all-gather(f32[4,32,128]{2,1,0:T(8,128)} %all-reduce.8.cloned.1.call-done), channel_id=3, replica_groups=mesh['layer'=2,'row'=4,'col'=4] {'row'}, dimensions={1}, use_global_device_ids=true | all-gather | bytes 327680 | tf_op jit(solution)/shard_map/all_gather | solution.py:52
  93.8 31.8 %all-reduce.10.cloned.1.call-done = f32[4,32,128]{2,0,1:T(4,128)} async-done(((f32[4,32,128]{2,0,1:T(4,128)}), f32[4,32,128]{2,0,1:T(4,128)}) %all-reduce.10.cloned.1.call-update) | async-done | bytes 65552 | tf_op jit(solution)/shard_map/psum | solution.py:36
  125.5 0.9 slice_subtract_fusion.2
  126.4 13.9 %all-gather.2 = f32[4,128,128]{2,0,1:T(4,128)S(1)} all-gather(f32[4,32,128]{2,0,1:T(4,128)S(1)} %slice_subtract_fusion.2), channel_id=4, replica_groups=mesh['layer'=2,'row'=4,'col'=4] {'row'}, dimensions={1}, use_global_device_ids=true | all-gather | bytes 327680 | tf_op jit(solution)/shard_map/all_gather | solution.py:38
  140.3 2.9 convolution_bitcast_fusion.2
  143.3 31.8 %all-reduce.12.cloned.1.call-done = f32[4,32,128]{2,1,0:T(8,128)} async-done(((f32[4,32,128]{2,1,0:T(8,128)}), f32[4,32,128]{2,1,0:T(8,128)}) %all-reduce.12.cloned.1.call-update) | async-done | bytes 65552 | tf_op jit(solution)/shard_map/psum | solution.py:50
  175.0 14.2 %all-gather.3 = f32[4,128,128]{2,1,0:T(8,128)S(1)} all-gather(f32[4,32,128]{2,1,0:T(8,128)} %all-reduce.12.cloned.1.call-done), channel_id=5, replica_groups=mesh['layer'=2,'row'=4,'col'=4] {'row'}, dimensions={1}, use_global_device_ids=true | all-gather | bytes 327680 | tf_op jit(solution)/shard_map/all_gather | solution.py:52
  191.6 31.8 %all-reduce.14.cloned.1.call-done = f32[4,32,128]{2,0,1:T(4,128)} async-done(((f32[4,32,128]{2,0,1:T(4,128)}), f32[4,32,128]{2,0,1:T(4,128)}) %all-reduce.14.cloned.1.call-update) | async-done | bytes 65552 | tf_op jit(solution)/shard_map/psum | solution.py:36
  224.2 13.9 %all-gather.4 = f32[4,128,128]{2,0,1:T(4,128)S(1)} all-gather(f32[4,32,128]{2,0,1:T(4,128)S(1)} %slice_subtract_fusion.1), channel_id=6, replica_groups=mesh['layer'=2,'row'=4,'col'=4] {'row'}, dimensions={1}, use_global_device_ids=true | all-gather | bytes 327680 | tf_op jit(solution)/shard_map/all_gather | solution.py:38
  238.1 2.9 convolution_bitcast_fusion.1
  241.1 31.8 %all-reduce.16.cloned.1.call-done = f32[4,32,128]{2,1,0:T(8,128)} async-done(((f32[4,32,128]{2,1,0:T(8,128)}), f32[4,32,128]{2,1,0:T(8,128)}) %all-reduce.16.cloned.1.call-update) | async-done | bytes 65552 | tf_op jit(solution)/shard_map/psum | solution.py:50
  272.8 14.1 %all-gather.5 = f32[4,128,128]{2,1,0:T(8,128)S(1)} all-gather(f32[4,32,128]{2,1,0:T(8,128)} %all-reduce.16.cloned.1.call-done), channel_id=7, replica_groups=mesh['layer'=2,'row'=4,'col'=4] {'row'}, dimensions={1}, use_global_device_ids=true | all-gather | bytes 327680 | tf_op jit(solution)/shard_map/all_gather | solution.py:52
  289.3 31.8 %all-reduce.18.cloned.1.call-done = f32[4,32,128]{2,0,1:T(4,128)} async-done(((f32[4,32,128]{2,0,1:T(4,128)}), f32[4,32,128]{2,0,1:T(4,128)}) %all-reduce.18.cloned.1.call-update) | async-done | bytes 65552 | tf_op jit(solution)/shard_map/psum | solution.py:36
  321.1 0.9 slice_subtract_fusion
  321.9 13.9 %all-gather.6 = f32[4,128,128]{2,0,1:T(4,128)S(1)} all-gather(f32[4,32,128]{2,0,1:T(4,128)S(1)} %slice_subtract_fusion), channel_id=8, replica_groups=mesh['layer'=2,'row'=4,'col'=4] {'row'}, dimensions={1}, use_global_device_ids=true | all-gather | bytes 327680 | tf_op jit(solution)/shard_map/all_gather | solution.py:38
  335.8 2.9 convolution_bitcast_fusion
  338.7 31.8 %all-reduce.20.cloned.1.call-done = f32[4,32,128]{2,1,0:T(8,128)} async-done(((f32[4,32,128]{2,1,0:T(8,128)}), f32[4,32,128]{2,1,0:T(8,128)}) %all-reduce.20.cloned.1.call-update) | async-done | bytes 65552 | tf_op jit(solution)/shard_map/psum | solution.py:50
  370.5 1.6 maximum_bitcast_fusion
  (46 shorter events, 10.2 us)
Async XLA Ops:
  6.5 85.4 %copy-start = (f32[1,1,4,128,128]{4,3,2,1,0:T(8,128)S(1)}, f32[1,1,4,128,128]{4,3,2,1,0:T(8,128)}, u32[]{:S(2)}) copy-start(f32[1,1,4,128,128]{4,3,2,1,0:T(8,128)} %param.11) | copy-start | bytes 786436
  6.5 20.4 %reduce-scatter.2.cloned.1.call-start = ((), (), s32[]{:S(2)}) async-start(), calls=%async_computation.1 | async-start | bytes 786432 | tf_op jit(solution)/shard_map/reduce_scatter | solution.py:27
  8.7 68.6 %all-reduce.8.cloned.1.call-start = ((), (), s32[]{:S(2)}) async-start(), calls=%async_computation.2 | async-start | bytes 131072 | tf_op jit(solution)/shard_map/psum | solution.py:50
  45.0 80.5 %all-reduce.10.cloned.1.call-start = ((), (), s32[]{:S(2)}) async-start(), calls=%async_computation.3 | async-start | bytes 131072 | tf_op jit(solution)/shard_map/psum | solution.py:36
  93.7 81.3 %all-reduce.12.cloned.1.call-start = ((), (), s32[]{:S(2)}) async-start(), calls=%async_computation.4 | async-start | bytes 131072 | tf_op jit(solution)/shard_map/psum | solution.py:50
  140.3 230.3 %copy-start.1 = (f32[4,32,128]{2,1,0:T(8,128)S(1)}, f32[4,32,128]{2,1,0:T(8,128)}, u32[]{:S(2)}) copy-start(f32[4,32,128]{2,1,0:T(8,128)} %all-reduce.8.cloned.1.call-done) | copy-start | bytes 196612
  143.2 80.2 %all-reduce.14.cloned.1.call-start = ((), (), s32[]{:S(2)}) async-start(), calls=%async_computation.5 | async-start | bytes 131072 | tf_op jit(solution)/shard_map/psum | solution.py:36
  175.0 195.5 %copy-start.2 = (f32[4,32,128]{2,1,0:T(8,128)S(1)}, f32[4,32,128]{2,1,0:T(8,128)}, u32[]{:S(2)}) copy-start(f32[4,32,128]{2,1,0:T(8,128)} %all-reduce.12.cloned.1.call-done) | copy-start | bytes 196612
  191.6 81.3 %all-reduce.16.cloned.1.call-start = ((), (), s32[]{:S(2)}) async-start(), calls=%async_computation.6 | async-start | bytes 131072 | tf_op jit(solution)/shard_map/psum | solution.py:50
  241.0 80.1 %all-reduce.18.cloned.1.call-start = ((), (), s32[]{:S(2)}) async-start(), calls=%async_computation.7 | async-start | bytes 131072 | tf_op jit(solution)/shard_map/psum | solution.py:36
  289.3 81.3 %all-reduce.20.cloned.1.call-start = ((), (), s32[]{:S(2)}) async-start(), calls=%async_computation.8 | async-start | bytes 131072 | tf_op jit(solution)/shard_map/psum | solution.py:50
Sparse Core Ops, SparseCore 0:
  9.6 17.3 reduce-scatter.1
  45.1 32.1 all-reduce.7
  93.8 31.6 all-reduce.9
  143.3 31.6 all-reduce.11
  191.7 31.6 all-reduce.13
  241.1 31.6 all-reduce.15
  289.4 31.6 all-reduce.17
  338.8 31.6 all-reduce.19
where the time goes:
time: 380 us; the launch traced here: 379 us
  waiting for transfers between devices  239 us (63%)
  blocking collectives  97.8 us (26%)
  matrix products  14.9 us (4%)
  between operations  13.6 us (4%)
  other arithmetic  8.02 us (2%)
  local copies, waits for them, and re-layouts  5.16 us (1%)
    psum x4, waiting for transfers between devices, body(): solved_own = lax.psum(partial_solved, 'col')  128 us
    psum x3, waiting for transfers between devices, body(): summed = lax.psum(accumulated[first_row:last_row], 'col')  95.3 us
    all_gather x4, blocking collectives, body(): lax.all_gather(target_rows[:, None], 'row', axis=1, tiled=True)  55.5 us
    all_gather x3, blocking collectives, body(): lax.all_gather(solved_own[:, None], 'row', axis=1, tiled=True)  42.3 us
    reduce_scatter x1, waiting for transfers between devices, body(): lax.psum_scatter(below[0, :, 0], 'layer', scatter_dimension=1, tiled=True)  16.2 us
    dot_general x4, matrix products, body(): jnp.einsum('exnc,xvc->evn', inverted_diagonal[current_supernode], local_t...  11.6 us
  transfers between devices with their start and end apart: 8, of which 8 were waited for; matrix products, arithmetic and copies ran while one was open for 1% of the time, Pallas kernels for 0%

commit v1 on v0

--- a/solution.py
+++ b/solution.py
@@ -33,7 +33,7 @@
         merged_part = merged[first_row:last_row]
         offset = col_index - current_supernode * NB
         active = ((offset >= 0) & (offset < NB)).astype(jnp.float32)
-        summed = lax.psum(accumulated[first_row:last_row], "col")
+        summed = jnp.sum(lax.all_gather(accumulated[first_row:last_row], "col"), axis=0)
         target_rows = merged_part - summed
         relayed = lax.all_gather(target_rows[:, None], "row", axis=1, tiled=True).reshape(
             NB, rhs_width, BLK

time: 380 us -> 299 us (0.79)
  waiting for transfers between devices: 239 us -> 146 us
  blocking collectives: 97.8 us -> 115 us
    psum x3 -> x0, waiting for transfers between devices: 95.3 us -> none  [body(): summed = lax.psum(accumulated[first_row:last_row], 'col')]
    all_gather x0 -> x3, blocking collectives: none -> 17.3 us  [body(): lax.all_gather(accumulated[first_row:last_row], 'col')]
  transfers between devices with their start and end apart: 8 -> 5, of which waited for: 8 -> 5; matrix products, arithmetic and copies ran while one was open for 1% -> 1% of each run, Pallas kernels for 0% -> 0%
where the time goes in v1:
time: 299 us; the launch traced here: 298 us
  waiting for transfers between devices  146 us (49%)
  blocking collectives  115 us (38%)
  matrix products  14.9 us (5%)
  between operations  13.3 us (4%)
  other arithmetic  5.04 us (2%)
  local copies, waits for them, and re-layouts  3.93 us (1%)
    psum x4, waiting for transfers between devices, body(): solved_own = lax.psum(partial_solved, 'col')  129 us
    all_gather x4, blocking collectives, body(): lax.all_gather(target_rows[:, None], 'row', axis=1, tiled=True)  55.5 us
    all_gather x3, blocking collectives, body(): lax.all_gather(solved_own[:, None], 'row', axis=1, tiled=True)  42.3 us
    all_gather x3, blocking collectives, body(): lax.all_gather(accumulated[first_row:last_row], 'col')  17.3 us
    reduce_scatter x1, waiting for transfers between devices, body(): lax.psum_scatter(below[0, :, 0], 'layer', scatter_dimension=1, tiled=True)  16.2 us
    dot_general x4, matrix products, body(): jnp.einsum('exnc,xvc->evn', inverted_diagonal[current_supernode], local_t...  11.6 us
  transfers between devices with their start and end apart: 5, of which 5 were waited for; matrix products, arithmetic and copies ran while one was open for 1% of the time, Pallas kernels for 0%

profile of v1, /device:TPU:0, one launch (start us, length us, event | category | flops | bytes accessed | tf_op | source)
XLA Modules:
  0.0 298.2 jit_solution(11721482311236933981)
XLA Ops:
  6.5 2.2 copy.83
  8.8 0.7 and_select_fusion
  10.1 0.7 compare_and_fusion
  10.8 16.2 %reduce-scatter.2.cloned.1.call-done = f32[16,32,128]{2,0,1:T(8,128)} async-done(((f32[16,64,128]{2,0,1:T(8,128)}), f32[16,32,128]{2,0,1:T(8,128)}) %reduce-scatter.2.cloned.1.call-update) | async-done | bytes 262160 | tf_op jit(solution)/shard_map/reduce_scatter | solution.py:27
  27.0 1.2 bitcast_subtract_fusion
  28.2 13.9 %all-gather = f32[4,128,128]{2,0,1:T(4,128)S(1)} all-gather(f32[4,32,128]{2,0,1:T(4,128)S(1)} %slice.54), channel_id=2, replica_groups=mesh['layer'=2,'row'=4,'col'=4] {'row'}, dimensions={1}, use_global_device_ids=true | all-gather | bytes 327680 | tf_op jit(solution)/shard_map/all_gather | solution.py:38
  42.1 2.9 convolution_bitcast_fusion.3
  45.1 32.2 %all-reduce.5.cloned.1.call-done = f32[4,32,128]{2,1,0:T(8,128)} async-done(((f32[4,32,128]{2,1,0:T(8,128)}), f32[4,32,128]{2,1,0:T(8,128)}) %all-reduce.5.cloned.1.call-update) | async-done | bytes 65552 | tf_op jit(solution)/shard_map/psum | solution.py:50
  77.3 14.1 %all-gather.1 = f32[4,128,128]{2,1,0:T(8,128)S(1)} all-gather(f32[4,32,128]{2,1,0:T(8,128)} %all-reduce.5.cloned.1.call-done), channel_id=3, replica_groups=mesh['layer'=2,'row'=4,'col'=4] {'row'}, dimensions={1}, use_global_device_ids=true | all-gather | bytes 327680 | tf_op jit(solution)/shard_map/all_gather | solution.py:52
  93.1 5.8 %all-gather.2 = f32[16,32,128]{2,1,0:T(8,128)S(1)} all-gather(f32[4,32,128]{2,1,0:T(8,128)S(1)} %copy.38), channel_id=4, replica_groups=mesh['layer'=2,'row'=4,'col'=4] {'col'}, dimensions={0}, use_global_device_ids=true | all-gather | bytes 327680 | tf_op jit(solution)/shard_map/all_gather | solution.py:36
  98.9 13.9 %all-gather.3 = f32[4,128,128]{2,0,1:T(4,128)S(1)} all-gather(f32[4,32,128]{2,0,1:T(4,128)S(1)} %slice_subtract_fusion.2), channel_id=5, replica_groups=mesh['layer'=2,'row'=4,'col'=4] {'row'}, dimensions={1}, use_global_device_ids=true | all-gather | bytes 327680 | tf_op jit(solution)/shard_map/all_gather | solution.py:38
  112.8 2.9 convolution_bitcast_fusion.2
  115.8 32.4 %all-reduce.7.cloned.1.call-done = f32[4,32,128]{2,1,0:T(8,128)} async-done(((f32[4,32,128]{2,1,0:T(8,128)}), f32[4,32,128]{2,1,0:T(8,128)}) %all-reduce.7.cloned.1.call-update) | async-done | bytes 65552 | tf_op jit(solution)/shard_map/psum | solution.py:50
  148.2 14.2 %all-gather.4 = f32[4,128,128]{2,1,0:T(8,128)S(1)} all-gather(f32[4,32,128]{2,1,0:T(8,128)} %all-reduce.7.cloned.1.call-done), channel_id=6, replica_groups=mesh['layer'=2,'row'=4,'col'=4] {'row'}, dimensions={1}, use_global_device_ids=true | all-gather | bytes 327680 | tf_op jit(solution)/shard_map/all_gather | solution.py:52
  164.1 5.8 %all-gather.5 = f32[16,32,128]{2,1,0:T(8,128)S(1)} all-gather(f32[4,32,128]{2,1,0:T(8,128)S(1)} %copy.43), channel_id=7, replica_groups=mesh['layer'=2,'row'=4,'col'=4] {'col'}, dimensions={0}, use_global_device_ids=true | all-gather | bytes 327680 | tf_op jit(solution)/shard_map/all_gather | solution.py:36
  169.9 13.9 %all-gather.6 = f32[4,128,128]{2,0,1:T(4,128)S(1)} all-gather(f32[4,32,128]{2,0,1:T(4,128)S(1)} %slice_subtract_fusion.1), channel_id=8, replica_groups=mesh['layer'=2,'row'=4,'col'=4] {'row'}, dimensions={1}, use_global_device_ids=true | all-gather | bytes 327680 | tf_op jit(solution)/shard_map/all_gather | solution.py:38
  183.8 2.9 convolution_bitcast_fusion.1
  186.8 32.4 %all-reduce.9.cloned.1.call-done = f32[4,32,128]{2,1,0:T(8,128)} async-done(((f32[4,32,128]{2,1,0:T(8,128)}), f32[4,32,128]{2,1,0:T(8,128)}) %all-reduce.9.cloned.1.call-update) | async-done | bytes 65552 | tf_op jit(solution)/shard_map/psum | solution.py:50
  219.2 14.1 %all-gather.7 = f32[4,128,128]{2,1,0:T(8,128)S(1)} all-gather(f32[4,32,128]{2,1,0:T(8,128)} %all-reduce.9.cloned.1.call-done), channel_id=9, replica_groups=mesh['layer'=2,'row'=4,'col'=4] {'row'}, dimensions={1}, use_global_device_ids=true | all-gather | bytes 327680 | tf_op jit(solution)/shard_map/all_gather | solution.py:52
  235.0 5.8 %all-gather.8 = f32[16,32,128]{2,1,0:T(8,128)S(1)} all-gather(f32[4,32,128]{2,1,0:T(8,128)S(1)} %copy.48), channel_id=10, replica_groups=mesh['layer'=2,'row'=4,'col'=4] {'col'}, dimensions={0}, use_global_device_ids=true | all-gather | bytes 327680 | tf_op jit(solution)/shard_map/all_gather | solution.py:36
  240.8 13.9 %all-gather.9 = f32[4,128,128]{2,0,1:T(4,128)S(1)} all-gather(f32[4,32,128]{2,0,1:T(4,128)S(1)} %slice_subtract_fusion), channel_id=11, replica_groups=mesh['layer'=2,'row'=4,'col'=4] {'row'}, dimensions={1}, use_global_device_ids=true | all-gather | bytes 327680 | tf_op jit(solution)/shard_map/all_gather | solution.py:38
  254.7 2.9 convolution_bitcast_fusion
  257.6 32.4 %all-reduce.11.cloned.1.call-done = f32[4,32,128]{2,1,0:T(8,128)} async-done(((f32[4,32,128]{2,1,0:T(8,128)}), f32[4,32,128]{2,1,0:T(8,128)}) %all-reduce.11.cloned.1.call-update) | async-done | bytes 65552 | tf_op jit(solution)/shard_map/psum | solution.py:50
  290.0 1.6 maximum_bitcast_fusion
  (46 shorter events, 6.2 us)
Async XLA Ops:
  6.5 85.4 %copy-start = (f32[1,1,4,128,128]{4,3,2,1,0:T(8,128)S(1)}, f32[1,1,4,128,128]{4,3,2,1,0:T(8,128)}, u32[]{:S(2)}) copy-start(f32[1,1,4,128,128]{4,3,2,1,0:T(8,128)} %param.11) | copy-start | bytes 786436
  6.5 20.4 %reduce-scatter.2.cloned.1.call-start = ((), (), s32[]{:S(2)}) async-start(), calls=%async_computation.1 | async-start | bytes 786432 | tf_op jit(solution)/shard_map/reduce_scatter | solution.py:27
  8.7 68.6 %all-reduce.5.cloned.1.call-start = ((), (), s32[]{:S(2)}) async-start(), calls=%async_computation.2 | async-start | bytes 131072 | tf_op jit(solution)/shard_map/psum | solution.py:50
  45.0 103.2 %all-reduce.7.cloned.1.call-start = ((), (), s32[]{:S(2)}) async-start(), calls=%async_computation.3 | async-start | bytes 131072 | tf_op jit(solution)/shard_map/psum | solution.py:50
  115.7 174.3 %copy-start.1 = (f32[4,32,128]{2,1,0:T(8,128)S(1)}, f32[4,32,128]{2,1,0:T(8,128)}, u32[]{:S(2)}) copy-start(f32[4,32,128]{2,1,0:T(8,128)} %all-reduce.5.cloned.1.call-done) | copy-start | bytes 196612
  115.8 103.4 %all-reduce.9.cloned.1.call-start = ((), (), s32[]{:S(2)}) async-start(), calls=%async_computation.4 | async-start | bytes 131072 | tf_op jit(solution)/shard_map/psum | solution.py:50
  148.2 141.9 %copy-start.2 = (f32[4,32,128]{2,1,0:T(8,128)S(1)}, f32[4,32,128]{2,1,0:T(8,128)}, u32[]{:S(2)}) copy-start(f32[4,32,128]{2,1,0:T(8,128)} %all-reduce.7.cloned.1.call-done) | copy-start | bytes 196612
  186.7 103.3 %all-reduce.11.cloned.1.call-start = ((), (), s32[]{:S(2)}) async-start(), calls=%async_computation.5 | async-start | bytes 131072 | tf_op jit(solution)/shard_map/psum | solution.py:50
Sparse Core Ops, SparseCore 0:
  9.6 17.3 reduce-scatter.1
  45.1 32.1 all-reduce.4
  115.9 32.2 all-reduce.6
  186.9 32.2 all-reduce.8
  257.7 32.2 all-reduce.10
